TPU v7x, 128 devices: a whole 4x4x4 slice. The times are simulated.
128 devices in a mesh: fsdp: 4 (over z_hi, core), ctx: 32 (over z_lo, x, y).
Axes of the slice: x: 4, y: 4, z: 4 (z_hi: 2, z_lo: 2; z = z_hi * 2 + z_lo), core: 2. Of those that a mesh axis runs over, the one named last changes fastest.
Arguments:
- tokens: bfloat16 [4, 16384, 8192], P('fsdp', 'ctx'), may hold values from -56 to 56
- codes: int32 [128, 20480], P('fsdp'), may hold values from 0 to 65535
- scales: bfloat16 [128, 1280], P('fsdp'), may hold values from 0.0039978027 to 0.039794922
- down_adapter_matrix: bfloat16 [128, 4096], P('fsdp'), may hold values from -0.0625 to 0.0625
- up_adapter_matrix: bfloat16 [64, 1280], replicated, may hold values from -0.75 to 0.75
- positions: int32 [4, 16384], P('fsdp', 'ctx'), may hold values from 0 to 16383, as said below
Outputs:
- attended: bfloat16 [4, 16384, 1024], P('fsdp', 'ctx')
Inputs may be any that keep to these rules, and one draw needn't show every extreme that they name: In each sequence the first and the last 256 tokens of each device's share hold consecutive increasing positions, of some block a and of block 63 - a of the sequence (blocks of 256 positions), a different a on each device of a sequence; every position of 0 to 16383 appears once in each sequence.
All inputs are finite; a program needn't handle non-finite values.
Results may differ from a plain program's by a relative error of at most 0.014.
Values may be sent and summed in bfloat16 or wider, within the bound.
A program may use at most 192 MiB of HBM per device.

v0:
```python
import jax
import jax.numpy as jnp
from jax import lax
from jax.sharding import PartitionSpec as P

QH = 8
HD = 128
normal_float_levels = [
    -1.0,
    -0.6961928009986877,
    -0.5250730514526367,
    -0.39491748809814453,
    -0.28444138169288635,
    -0.18477343022823334,
    -0.09105003625154495,
    0.0,
    0.07958029955625534,
    0.16093020141124725,
    0.24611230194568634,
    0.33791524171829224,
    0.44070982933044434,
    0.5626170039176941,
    0.7229568362236023,
    1.0,
]
rope_base = 500000.0
adapter_scaling = 0.5


def unpack_codes(packed):
    blocks = packed.shape[0]
    words = packed.reshape(blocks, 64, -1)
    nibbles = [jnp.remainder(jnp.floor_divide(words, 16**place), 16) for place in range(4)]
    return jnp.stack(nibbles, axis=-1).reshape(blocks, 64, -1)


def pick_level(code_full):
    bit_flags = [jnp.remainder(jnp.floor_divide(code_full, 2**place), 2) == 1 for place in range(4)]
    current = [jnp.float32(level) for level in normal_float_levels]
    for place in range(4):
        current = [
            jnp.where(bit_flags[place], current[2 * pair + 1], current[2 * pair])
            for pair in range(len(current) // 2)
        ]
    return current[0]


def dequantize(packed, block_scales):
    code_full = unpack_codes(packed)
    values = pick_level(code_full)
    scaled = values * block_scales.astype(jnp.float32)[:, None, :]
    return scaled.reshape(-1, scaled.shape[-1]).astype(jnp.bfloat16)


def rotate_pairs(values, angles):
    half_size = values.shape[-1] // 2
    first_half = values[..., :half_size]
    second_half = values[..., half_size:]
    cosine = jnp.cos(angles)
    sine = jnp.sin(angles)
    return jnp.concatenate(
        [first_half * cosine - second_half * sine, second_half * cosine + first_half * sine],
        axis=-1,
    )


def make_angles(token_position):
    half_size = HD // 2
    steps_idx = jnp.arange(half_size, dtype=jnp.float32)
    inverse = jnp.exp(-jnp.log(jnp.float32(rope_base)) * 2.0 * steps_idx / HD)
    return token_position.astype(jnp.float32)[:, None] * inverse[None, :]


def tile_update(state, query_part, query_pos, tile, tile_pos):
    running_max, running_sum, running_acc = state
    scores = jnp.einsum("hqd,kd->hqk", query_part, tile[:, :HD], preferred_element_type=jnp.float32)
    scores = jnp.where(tile_pos[None, None, :] <= query_pos[None, :, None], scores, -jnp.inf)
    new_max = jnp.maximum(running_max, jnp.max(scores, axis=-1))
    factor = jnp.exp(running_max - new_max)
    expo = jnp.exp(scores - new_max[..., None])
    new_sum = running_sum * factor + jnp.sum(expo, axis=-1)
    weights = expo.astype(jnp.bfloat16)
    new_acc = running_acc * factor[..., None] + jnp.einsum(
        "hqk,kd->hqd", weights, tile[:, HD:], preferred_element_type=jnp.float32
    )
    return (new_max, new_sum, new_acc)


def on_device(tokens, codes, scales, down_adapter_matrix, up_adapter_matrix, positions):
    local_tokens = tokens[0]
    local_pos = positions[0]
    tok_count = local_tokens.shape[0]
    adapter_rank_size = up_adapter_matrix.shape[0]
    input_width = up_adapter_matrix.shape[1]
    own_weight = dequantize(codes, scales).reshape(scales.shape[0], 64 * input_width)
    weight_piece = lax.all_gather(own_weight, "fsdp", axis=0, tiled=True)
    adapter_slice = lax.all_gather(down_adapter_matrix, "fsdp", axis=0, tiled=True)
    rows = weight_piece.shape[0] * 64
    first_total = jnp.dot(
        local_tokens, weight_piece.reshape(rows, input_width), preferred_element_type=jnp.float32
    )
    second_total = jnp.dot(
        local_tokens,
        adapter_slice.reshape(rows, adapter_rank_size),
        preferred_element_type=jnp.float32,
    )
    low_rank_output = second_total.astype(jnp.bfloat16)
    joined_output = first_total + adapter_scaling * jnp.dot(
        low_rank_output, up_adapter_matrix, preferred_element_type=jnp.float32
    )
    angles = make_angles(local_pos)
    qwidth = QH * HD
    query_output = joined_output[:, :qwidth].reshape(tok_count, QH, HD).transpose(1, 0, 2)
    query_output = (rotate_pairs(query_output, angles) * HD ** (-0.5)).astype(jnp.bfloat16)
    key = rotate_pairs(joined_output[:, qwidth : qwidth + HD], angles).astype(jnp.bfloat16)
    value_output = joined_output[:, qwidth + HD :].astype(jnp.bfloat16)
    keys_values = jnp.concatenate([key, value_output], axis=1)
    all_positions = lax.all_gather(local_pos, "ctx", axis=0, tiled=True)
    half_size = tok_count // 2
    query_parts = (query_output[:, :half_size], query_output[:, half_size:])
    pos_parts = (local_pos[:half_size], local_pos[half_size:])
    empty_state = (
        jnp.full((QH, half_size), -1e30, jnp.float32),
        jnp.zeros((QH, half_size), jnp.float32),
        jnp.zeros((QH, half_size, HD), jnp.float32),
    )
    states = (empty_state, empty_state)
    piece = lax.all_gather(keys_values, "ctx", axis=0, tiled=True)
    count = piece.shape[0]

    def one_tile(carry, tile_idx):
        tile = lax.dynamic_slice_in_dim(piece, tile_idx * half_size, half_size, 0)
        tile_pos = lax.dynamic_slice_in_dim(all_positions, tile_idx * half_size, half_size, 0)
        updated = []
        for part_idx in range(2):

            def apply_tile(state, part_idx=part_idx):
                return tile_update(
                    state, query_parts[part_idx], pos_parts[part_idx], tile, tile_pos
                )

            def keep_state(state):
                return state

            visible = jnp.min(tile_pos) <= jnp.max(pos_parts[part_idx])
            updated.append(lax.cond(visible, apply_tile, keep_state, carry[part_idx]))
        return ((updated[0], updated[1]), None)

    states, unused = lax.scan(one_tile, states, jnp.arange(count // half_size, dtype=jnp.int32))
    halves = [states[part_idx][2] / states[part_idx][1][..., None] for part_idx in range(2)]
    combined = jnp.concatenate(halves, axis=1)
    attended = combined.transpose(1, 0, 2).reshape(tok_count, QH * HD).astype(jnp.bfloat16)
    return attended[None]


def solution(mesh):
    in_specs = (
        P("fsdp", "ctx", None),
        P("fsdp", None),
        P("fsdp", None),
        P("fsdp", None),
        P(),
        P("fsdp", "ctx"),
    )
    out_specs = P("fsdp", "ctx", None)
    return jax.shard_map(
        on_device, mesh=mesh, in_specs=in_specs, out_specs=out_specs, check_vma=False
    )
```

profile of v0, /device:TPU:0, one launch (start us, length us, event | category | flops | bytes accessed | tf_op | source)
XLA Modules:
  0.0 1176.6 jit_solution(5774909089922595813)
XLA Ops:
  7.3 2.8 reshape.460
  10.1 8.5 add_select_fusion.13
  18.6 5.6 pad_add_fusion
  24.2 28.0 %copy.44 = s32[32,64,320,4]{0,3,2,1:T(4,128)} copy(s32[32,64,320,4]{2,1,3,0:T(8,128)} %pad_add_fusion) | data formatting | bytes 20971520 | tf_op jit(solution)/shard_map/stack | solution.py:34
  52.4 151.2 %fusion.33 = bf16[32,81920]{0,1:T(8,128)(2,1)} fusion(s32[32,81920]{0,1:T(8,128)} %bitcast.50, f32[32,1280]{0,1:T(8,128)S(1)} %copy.45), kind=kLoop, calls=%fused_computation.65 | loop fusion | flops 243793920 | bytes 15892480 | tf_op jit(solution)/shard_map/convert_element_type | solution.py:52
  203.6 17.3 %copy.46 = bf16[32,81920]{1,0:T(8,128)(2,1)} copy(bf16[32,81920]{0,1:T(8,128)(2,1)} %fusion.33) | data formatting | bytes 10485760 | tf_op jit(solution)/shard_map/convert_element_type | solution.py:52
  221.7 4.3 reshape.463
  225.9 133.4 %all-gather.5.cloned.1.call-done = bf16[128,81920]{1,0:T(8,128)(2,1)} async-done(((bf16[32,81920]{1,0:T(8,128)(2,1)}), bf16[128,81920]{1,0:T(8,128)(2,1)}) %all-gather.5.cloned.1.call-update) | async-done | bytes 20971536 | tf_op jit(solution)/shard_map/all_gather | solution.py:96
  359.4 23.6 %reshape.462 = bf16[8192,1280]{1,0:T(8,128)(2,1)} reshape(bf16[128,81920]{1,0:T(8,128)(2,1)} %all-gather.5.cloned.1.call-done) | data formatting | bytes 41943040 | tf_op jit(solution)/shard_map/reshape | solution.py:100
  383.0 18.7 %fusion.41 = f32[512,1280]{0,1:T(8,128)} fusion(bf16[8192,1280]{1,0:T(8,128)(2,1)} %reshape.462, bf16[1,512,8192]{2,1,0:T(8,128)(2,1)} %param.12), kind=kOutput, calls=%fused_computation.96 | convolution fusion | flops 10737418240 | bytes 31981568 | tf_op jit(solution)/shard_map/dot_general | solution.py:99
  401.7 7.9 fusion.40
  411.0 80.8 %all-gather = s32[1,16384]{1,0:T(1,128)S(1)} all-gather(s32[1,512]{1,0:T(1,128)S(1)} %copy-done.2), channel_id=2, replica_groups=mesh['fsdp'=4,'ctx'=32] {'ctx'}, dimensions={1}, use_global_device_ids=true | all-gather | bytes 67584 | tf_op jit(solution)/shard_map/all_gather | solution.py:118
  497.8 78.2 %all-gather.9.cloned.1.call-done = bf16[16384,256]{0,1:T(8,128)(2,1)} async-done(((bf16[512,256]{0,1:T(8,128)(2,1)}), bf16[16384,256]{0,1:T(8,128)(2,1)}) %all-gather.9.cloned.1.call-update) | async-done | bytes 8388624 | tf_op jit(solution)/shard_map/all_gather | solution.py:128
  576.2 591.1 %while.21 = (s32[]{:T(128)}, f32[8,256]{1,0:T(8,128)S(1)}, f32[8,256]{1,0:T(8,128)S(1)}, f32[8,256,128]{2,1,0:T(8,128)S(1)}, f32[8,256]{1,0:T(8,128)S(1)}, /*ind...) while((s32[]{:T(128)}, f32[8,256]{1,0:T(8,128)S(1)}, ...), condition=%wide.region_12.13_spmd, body=%wide.region_2.0_spmd.sunk | while | flops 546447616 | bytes 19405304 | solution.py:149
  582.1 2.0 conditional.5
  593.3 2.0 conditional.5
  611.7 2.0 conditional.5
  620.9 2.0 conditional.5
  630.1 2.0 conditional.5
  639.3 2.0 conditional.5
  648.5 2.0 conditional.5
  657.7 2.0 conditional.5
  666.9 2.0 conditional.5
  676.1 2.0 conditional.5
  685.3 2.0 conditional.5
  694.5 2.0 conditional.5
  703.8 2.0 conditional.5
  713.0 2.0 conditional.5
  722.2 2.0 conditional.5
  731.4 2.0 conditional.5
  759.0 2.0 conditional.5
  768.2 2.0 conditional.5
  777.4 2.0 conditional.5
  786.6 2.0 conditional.5
  823.4 2.0 conditional.5
  832.6 2.0 conditional.5
  841.8 2.0 conditional.5
  851.0 2.0 conditional.5
  860.2 2.0 conditional.5
  869.4 2.0 conditional.5
  878.6 2.0 conditional.5
  906.2 2.0 conditional.5
  915.5 2.0 conditional.5
  924.7 2.0 conditional.5
  933.9 2.0 conditional.5
  943.1 2.0 conditional.5
  952.3 2.0 conditional.5
  961.5 2.0 conditional.5
  970.7 2.0 conditional.5
  989.1 2.0 conditional.5
  998.3 2.0 conditional.5
  1007.5 2.0 conditional.5
  1025.9 2.0 conditional.5
  1035.1 2.0 conditional.5
  1044.3 2.0 conditional.5
  1053.5 2.0 conditional.5
  1062.7 2.0 conditional.5
  1071.9 2.0 conditional.5
  1081.1 2.0 conditional.5
  1117.9 2.0 conditional.5
  1127.1 2.0 conditional.5
  1136.4 2.0 conditional.5
  1145.6 2.0 conditional.5
  1154.8 2.0 conditional.5
  (827 shorter events, 420.5 us)
Async XLA Ops:
  6.5 395.2 %copy-start = (bf16[64,1280]{1,0:T(8,128)(2,1)S(1)}, bf16[64,1280]{1,0:T(8,128)(2,1)}, u32[]{:S(2)}) copy-start(bf16[64,1280]{1,0:T(8,128)(2,1)} %param.16) | copy-start | bytes 491524
  6.5 215.1 %all-gather.7.cloned.1.call-start = ((), (), s32[]{:S(2)}) async-start(), calls=%async_computation.1 | async-start | bytes 1310720 | tf_op jit(solution)/shard_map/all_gather | solution.py:97
  7.3 352.1 %all-gather.5.cloned.1.call-start = ((), (), s32[]{:S(2)}) async-start(), calls=%async_computation | async-start | bytes 26214400 | tf_op jit(solution)/shard_map/all_gather | solution.py:96
  24.2 28.0 %copy-start.1 = (bf16[32,1280]{1,0:T(8,128)(2,1)S(1)}, bf16[32,1280]{1,0:T(8,128)(2,1)}, u32[]{:S(2)}) copy-start(bf16[32,1280]{1,0:T(8,128)(2,1)} %param.14) | copy-start | bytes 245764
  220.9 0.7 copy-start.2
  221.0 355.1 %all-gather.9.cloned.1.call-start = ((), (), s32[]{:S(2)}) async-start(), calls=%async_computation.2 | async-start | bytes 8650752 | tf_op jit(solution)/shard_map/all_gather | solution.py:128
Sparse Core Ops, SparseCore 0:
  9.0 23.3 all-gather.6
  221.1 138.2 all-gather.4
  411.1 164.9 all-gather.8
where the time goes:
time: 1180 us
  local copies, waits for them, and re-layouts  285 us (24%)
  other arithmetic  251 us (21%)
  loops' own time  213 us (18%)
  waiting for transfers between devices  212 us (18%)
  matrix products  121 us (10%)
  blocking collectives  80.8 us (7%)
  between operations  13.3 us (1%)
    another operation x1, loops' own time, on_device(): lax.scan(one_tile, states, jnp.arange(count // half_size, dtype=jnp.int32))  208 us
    dynamic_slice x128, local copies, waits for them, and re-layouts, one_tile(): tile = lax.dynamic_slice_in_dim(piece, tile_idx * half_size, half_size, 0)  164 us
    convert_element_type x1, other arithmetic, dequantize(): return scaled.reshape(-1, scaled.shape[-1]).astype(jnp.bfloat16)  151 us
    all_gather x1, waiting for transfers between devices, on_device(): weight_piece = lax.all_gather(own_weight, 'fsdp', axis=0, tiled=True)  133 us
    all_gather x1, blocking collectives, on_device(): all_positions = lax.all_gather(local_pos, 'ctx', axis=0, tiled=True)  80.8 us
    all_gather x1, waiting for transfers between devices, on_device(): piece = lax.all_gather(keys_values, 'ctx', axis=0, tiled=True)  78.2 us
    dot_general x65, matrix products, tile_update(): jnp.einsum('hqk,kd->hqd', weights, tile[:, HD:], preferred_element_type=j...  65.4 us
    reduce_min x64, other arithmetic, one_tile(): visible = jnp.min(tile_pos) <= jnp.max(pos_parts[part_idx])  49.6 us
  transfers between devices with their start and end apart: 3, of which 2 were waited for; matrix products, arithmetic and copies ran while one was open for 19% of the time, Pallas kernels for 0%

commit v1 on v0

--- a/solution.py
+++ b/solution.py
@@ -125,7 +125,8 @@
         jnp.zeros((QH, half_size, HD), jnp.float32),
     )
     states = (empty_state, empty_state)
-    piece = lax.all_gather(keys_values, "ctx", axis=0, tiled=True)
+    sent = jnp.stack([keys_values] * lax.axis_size("ctx"))
+    piece = jnp.concatenate(lax.all_to_all(sent, "ctx", 0, 0), axis=0)
     count = piece.shape[0]
 
     def one_tile(carry, tile_idx):

time: 1180 us -> 1130 us (0.958)
  blocking collectives: 80.8 us -> 191 us
  local copies, waits for them, and re-layouts: 285 us -> 188 us
  waiting for transfers between devices: 212 us -> 135 us
    all_gather x1, blocking collectives: 80.8 us -> 191 us  [on_device(): all_positions = lax.all_gather(local_pos, 'ctx', axis=0, tiled=True)]
    dynamic_slice x128 -> x64, local copies, waits for them, and re-layouts: 164 us -> 58.4 us  [one_tile(): tile = lax.dynamic_slice_in_dim(piece, tile_idx * half_size, half_size, 0)]
    all_gather x1 -> x0, waiting for transfers between devices: 78.2 us -> none  [on_device(): piece = lax.all_gather(keys_values, 'ctx', axis=0, tiled=True)]
  transfers between devices with their start and end apart: 3 -> 3, of which waited for: 2 -> 1; matrix products, arithmetic and copies ran while one was open for 19% -> 20% of each run, Pallas kernels for 0% -> 0%
where the time goes in v1:
time: 1130 us; the launch traced here: 1120 us
  other arithmetic  251 us (22%)
  loops' own time  212 us (19%)
  blocking collectives  191 us (17%)
  local copies, waits for them, and re-layouts  188 us (17%)
  waiting for transfers between devices  135 us (12%)
  matrix products  122 us (11%)
  between operations  13.6 us (1%)
    another operation x1, loops' own time, on_device(): lax.scan(one_tile, states, jnp.arange(count // half_size, dtype=jnp.int32))  207 us
    all_gather x1, blocking collectives, on_device(): all_positions = lax.all_gather(local_pos, 'ctx', axis=0, tiled=True)  191 us
    convert_element_type x1, other arithmetic, dequantize(): return scaled.reshape(-1, scaled.shape[-1]).astype(jnp.bfloat16)  151 us
    all_gather x1, waiting for transfers between devices, on_device(): weight_piece = lax.all_gather(own_weight, 'fsdp', axis=0, tiled=True)  134 us
    dot_general x65, matrix products, tile_update(): jnp.einsum('hqk,kd->hqd', weights, tile[:, HD:], preferred_element_type=j...  65.4 us
    dynamic_slice x64, local copies, waits for them, and re-layouts, one_tile(): tile = lax.dynamic_slice_in_dim(piece, tile_idx * half_size, half_size, 0)  58.4 us
    reduce_min x64, other arithmetic, one_tile(): visible = jnp.min(tile_pos) <= jnp.max(pos_parts[part_idx])  47.4 us
    dynamic_slice x64, local copies, waits for them, and re-layouts, on_device(): lax.scan(one_tile, states, jnp.arange(count // half_size, dtype=jnp.int32))  39.7 us
  transfers between devices with their start and end apart: 3, of which 1 were waited for; matrix products, arithmetic and copies ran while one was open for 20% of the time, Pallas kernels for 0%

profile of v1, /device:TPU:0, one launch (start us, length us, event | category | flops | bytes accessed | tf_op | source)
XLA Modules:
  0.0 1119.6 jit_solution(454780429832980708)
XLA Ops:
  7.3 4.0 reshape.465
  11.3 9.6 add_select_fusion.13
  20.9 5.6 pad_add_fusion
  26.5 28.0 %copy.44 = s32[32,64,320,4]{0,3,2,1:T(4,128)} copy(s32[32,64,320,4]{2,1,3,0:T(8,128)} %pad_add_fusion) | data formatting | bytes 20971520 | tf_op jit(solution)/shard_map/stack | solution.py:34
  54.6 151.3 %fusion.33 = bf16[32,81920]{0,1:T(8,128)(2,1)} fusion(s32[32,81920]{0,1:T(8,128)} %bitcast.51, f32[32,1280]{0,1:T(8,128)S(1)} %copy.45), kind=kLoop, calls=%fused_computation.65 | loop fusion | flops 243793920 | bytes 15892480 | tf_op jit(solution)/shard_map/convert_element_type | solution.py:52
  205.9 17.3 %copy.46 = bf16[32,81920]{1,0:T(8,128)(2,1)} copy(bf16[32,81920]{0,1:T(8,128)(2,1)} %fusion.33) | data formatting | bytes 10485760 | tf_op jit(solution)/shard_map/convert_element_type | solution.py:52
  224.0 3.3 reshape.468
  227.2 134.4 %all-gather.4.cloned.1.call-done = bf16[128,81920]{1,0:T(8,128)(2,1)} async-done(((bf16[32,81920]{1,0:T(8,128)(2,1)}), bf16[128,81920]{1,0:T(8,128)(2,1)}) %all-gather.4.cloned.1.call-update) | async-done | bytes 20971536 | tf_op jit(solution)/shard_map/all_gather | solution.py:96
  361.7 23.6 %reshape.467 = bf16[8192,1280]{1,0:T(8,128)(2,1)} reshape(bf16[128,81920]{1,0:T(8,128)(2,1)} %all-gather.4.cloned.1.call-done) | data formatting | bytes 41943040 | tf_op jit(solution)/shard_map/reshape | solution.py:100
  385.3 18.7 %fusion.41 = f32[512,1280]{0,1:T(8,128)} fusion(bf16[8192,1280]{1,0:T(8,128)(2,1)} %reshape.467, bf16[1,512,8192]{2,1,0:T(8,128)(2,1)} %param.12), kind=kOutput, calls=%fused_computation.96 | convolution fusion | flops 10737418240 | bytes 31981568 | tf_op jit(solution)/shard_map/dot_general | solution.py:99
  404.0 8.8 fusion.40
  415.4 4.2 stack.5
  419.6 7.3 all-to-all-start
  426.9 190.6 %all-gather = s32[1,16384]{1,0:T(1,128)S(1)} all-gather(s32[1,512]{1,0:T(1,128)S(1)} %copy-done.2), channel_id=2, replica_groups=mesh['fsdp'=4,'ctx'=32] {'ctx'}, dimensions={1}, use_global_device_ids=true | all-gather | bytes 67584 | tf_op jit(solution)/shard_map/all_gather | solution.py:118
  618.2 3.1 slice.67
  621.6 2.1 copy.49
  625.6 484.4 %while.21 = (s32[]{:T(128)}, f32[8,256]{1,0:T(8,128)S(1)}, f32[8,256]{1,0:T(8,128)S(1)}, f32[8,256,128]{2,1,0:T(8,128)S(1)}, f32[8,256]{1,0:T(8,128)S(1)}, /*ind...) while((s32[]{:T(128)}, f32[8,256]{1,0:T(8,128)S(1)}, ...), condition=%wide.region_12.13_spmd, body=%wide.region_2.0_spmd.sunk | while | flops 546447616 | bytes 19143160 | solution.py:150
  629.8 2.0 conditional.5
  639.4 2.0 conditional.5
  646.9 2.0 conditional.5
  654.5 2.0 conditional.5
  662.0 2.0 conditional.5
  669.5 2.0 conditional.5
  677.1 2.0 conditional.5
  684.6 2.0 conditional.5
  692.1 2.0 conditional.5
  699.7 2.0 conditional.5
  707.2 2.0 conditional.5
  714.7 2.0 conditional.5
  722.3 2.0 conditional.5
  729.8 2.0 conditional.5
  737.4 2.0 conditional.5
  744.9 2.0 conditional.5
  752.4 2.0 conditional.5
  775.0 2.0 conditional.5
  782.6 2.0 conditional.5
  790.1 2.0 conditional.5
  797.7 2.0 conditional.5
  820.3 2.0 conditional.5
  827.8 2.0 conditional.5
  835.3 2.0 conditional.5
  842.9 2.0 conditional.5
  850.4 2.0 conditional.5
  857.9 2.0 conditional.5
  865.5 2.0 conditional.5
  873.0 2.0 conditional.5
  895.6 2.0 conditional.5
  903.2 2.0 conditional.5
  910.7 2.0 conditional.5
  918.2 2.0 conditional.5
  925.8 2.0 conditional.5
  933.3 2.0 conditional.5
  940.9 2.0 conditional.5
  948.4 2.0 conditional.5
  971.0 2.0 conditional.5
  978.5 2.0 conditional.5
  1001.1 2.0 conditional.5
  1008.7 2.0 conditional.5
  1016.2 2.0 conditional.5
  1023.8 2.0 conditional.5
  1031.3 2.0 conditional.5
  1038.8 2.0 conditional.5
  1061.4 2.0 conditional.5
  1069.0 2.0 conditional.5
  (764 shorter events, 318.9 us)
Async XLA Ops:
  6.5 397.4 %copy-start = (bf16[64,1280]{1,0:T(8,128)(2,1)S(1)}, bf16[64,1280]{1,0:T(8,128)(2,1)}, u32[]{:S(2)}) copy-start(bf16[64,1280]{1,0:T(8,128)(2,1)} %param.16) | copy-start | bytes 491524
  6.5 217.4 %all-gather.6.cloned.1.call-start = ((), (), s32[]{:S(2)}) async-start(), calls=%async_computation.2 | async-start | bytes 1310720 | tf_op jit(solution)/shard_map/all_gather | solution.py:97
  7.3 354.4 %all-gather.4.cloned.1.call-start = ((), (), s32[]{:S(2)}) async-start(), calls=%async_computation.1 | async-start | bytes 26214400 | tf_op jit(solution)/shard_map/all_gather | solution.py:96
  26.5 28.0 %copy-start.1 = (bf16[32,1280]{1,0:T(8,128)(2,1)S(1)}, bf16[32,1280]{1,0:T(8,128)(2,1)}, u32[]{:S(2)}) copy-start(bf16[32,1280]{1,0:T(8,128)(2,1)} %param.14) | copy-start | bytes 245764
  223.2 0.7 copy-start.2
  419.6 205.8 %all-to-all-start = ((bf16[32,512,256]{2,1,0:T(8,128)(2,1)}), bf16[32,512,256]{2,1,0:T(8,128)(2,1)}, u32[]{:S(2)}, u32[]{:S(2)}) async-start(bf16[32,512,256]{2,1,0:T(8,128)(2,1)} %stack.5), calls=%async_computation | async-start | bytes 16777216 | tf_op jit(solution)/shard_map/all_to_all | solution.py:129
Sparse Core Ops, SparseCore 0:
  9.0 23.3 all-gather.5
  223.4 138.2 all-gather.3
